TPU v7x, 32 devices: a whole 2x2x4 slice. The times are simulated.
32 devices in a mesh: frames: 8 (over y, x, core), chan: 4 (over z).
Axes of the slice: x: 2, y: 2, z: 4, core: 2. Of those that a mesh axis runs over, the one named last changes fastest.
Arguments:
- inputs: bfloat16 [16, 256, 16, 128], P('frames', 'chan'), may hold values from -6 to 6
- saved: bfloat16 [16, 256, 16, 128], P('frames', 'chan'), may hold values from -6 to 6
- cotangent: bfloat16 [8, 256, 512], P('frames', 'chan'), may hold values from -24 to 24
- spatial_w: bfloat16 [3, 3, 256, 256], P(None, None, 'chan'), may hold values from -0.125 to 0.125
- temporal_w: bfloat16 [3, 256, 256], replicated, may hold values from -0.21875 to 0.21875
Outputs:
- input_grad: bfloat16 [16, 256, 16, 128], P('frames', 'chan')
- spatial_grad: float32 [3, 3, 256, 256], P(None, None, 'chan')
- temporal_grad: float32 [3, 256, 256], P(None, 'chan')
All inputs are finite; a program needn't handle non-finite values.
Results may differ from a plain program's by a relative error of at most 0.0049.
Values may be sent and summed in bfloat16 or wider, within the bound.
No kernel may reach another device: no remote copies, remote signals or barrier semaphores. Data moves between devices by JAX's collectives and lax.ppermute only.
A program may use at most 64 MiB of HBM per device.

v0:
```python
import math
import jax
import jax.numpy as jnp
from jax import lax
from jax.sharding import PartitionSpec as P


def temporal_terms(saved_ext, grad_ext, temporal_w, row_total, frame_count):
    result = jnp.zeros((frame_count, row_total, grad_ext.shape[2]), jnp.float32)
    for tap in range(3):
        result = result + jnp.einsum(
            "fol,io->fil",
            grad_ext[2 - tap : 2 - tap + frame_count],
            temporal_w[tap],
            preferred_element_type=jnp.float32,
        )
    partial_value = jnp.stack(
        [
            jnp.einsum(
                "fil,fol->io",
                saved_ext[tap : tap + frame_count],
                grad_ext[1 : frame_count + 1],
                preferred_element_type=jnp.float32,
            )
            for tap in range(3)
        ]
    )
    return (result.astype(jnp.bfloat16), partial_value)


def shards(inputs, saved, cotangent, spatial_w, temporal_w):
    frame_count, quarter, row_count, col_count = inputs.shape
    channels = temporal_w.shape[1]
    row_half, col_half = (row_count // 2, col_count // 2)
    scale = 1.0 / math.sqrt(frame_count * lax.axis_size("frames") * row_count * col_count)
    full_cot = lax.all_gather(cotangent, "chan", axis=1, tiled=True)
    row_first, row_total = (0, channels)
    frame_pad = ((1, 1), (0, 0), (0, 0))
    pooled_saved = saved.reshape(frame_count, quarter, row_half, 2, col_half, 2).transpose(
        0, 1, 3, 5, 2, 4
    )
    pooled_saved = pooled_saved.reshape(frame_count, quarter, 4, row_half * col_half)
    pooled_cot = full_cot.reshape(1, channels, 1, row_half * col_half)
    moved_saved, moved_cot = (
        lax.all_to_all(pooled_saved, "frames", split_axis=3, concat_axis=0, tiled=True),
        lax.all_to_all(pooled_cot, "frames", split_axis=3, concat_axis=0, tiled=True),
    )
    frame_total, local_cells = (moved_saved.shape[0], moved_saved.shape[3])
    spread = jnp.broadcast_to(moved_cot[:, None], (frame_total // 2, 2, channels, 4, local_cells))
    upsampled = (
        spread.reshape(frame_total, channels, 4 * local_cells).astype(jnp.float32) * 0.125
    ).astype(jnp.bfloat16)
    grad_ext = jnp.pad(upsampled, frame_pad)
    saved_ext = jnp.pad(moved_saved.reshape(frame_total, quarter, 4 * local_cells), frame_pad)
    cell_grad, temporal_part = temporal_terms(
        saved_ext, grad_ext, temporal_w, row_total, frame_total
    )
    cell_grad = cell_grad.reshape(frame_total, row_total, 4, local_cells)
    back_grad = lax.all_to_all(cell_grad, "frames", split_axis=0, concat_axis=3, tiled=True)
    back_grad = back_grad.reshape(frame_count, row_total, 2, 2, row_half, col_half).transpose(
        0, 1, 4, 2, 5, 3
    )
    saved_grad = back_grad.reshape(frame_count, row_total, row_count, col_count)
    temporal_total = lax.psum(temporal_part, "frames")
    space_pad = ((0, 0), (0, 0), (1, 1), (1, 1))
    grad_pad = jnp.pad(saved_grad, space_pad)
    input_pad = jnp.pad(inputs, space_pad)
    input_sum = jnp.zeros((frame_count, quarter, row_count, col_count), jnp.float32)
    kernel_rows = []
    for tap_row in range(3):
        kernel_cols = []
        for tap_col in range(3):
            window = grad_pad[
                :, :, 2 - tap_row : 2 - tap_row + row_count, 2 - tap_col : 2 - tap_col + col_count
            ]
            input_sum = input_sum + jnp.einsum(
                "fohw,io->fihw",
                window,
                spatial_w[tap_row, tap_col],
                preferred_element_type=jnp.float32,
            )
            shifted = input_pad[:, :, tap_row : tap_row + row_count, tap_col : tap_col + col_count]
            kernel_cols.append(
                jnp.einsum("fihw,fohw->io", shifted, saved_grad, preferred_element_type=jnp.float32)
            )
        kernel_rows.append(jnp.stack(kernel_cols))
    spatial_part = jnp.stack(kernel_rows)
    spatial_total = lax.psum(spatial_part, "frames")
    return (input_sum.astype(jnp.bfloat16), spatial_total * scale, temporal_total * scale)


def solution(mesh):
    return jax.shard_map(
        shards,
        mesh=mesh,
        in_specs=(
            P("frames", "chan", None, None),
            P("frames", "chan", None, None),
            P("frames", "chan", None),
            P(None, None, "chan", None),
            P(),
        ),
        out_specs=(
            P("frames", "chan", None, None),
            P(None, None, "chan", None),
            P(None, "chan", None),
        ),
        check_vma=False,
    )
```

profile of v0, /device:TPU:0, one launch (start us, length us, event | category | flops | bytes accessed | tf_op | source)
XLA Modules:
  0.0 170.7 jit_solution(4398962847321769897)
XLA Ops:
  7.2 16.0 %all_gather.3 = bf16[1,256,512]{2,1,0:T(8,128)(2,1)S(1)} all-gather(bf16[1,64,512]{2,1,0:T(8,128)(2,1)} %param.7), channel_id=1, replica_groups=mesh['frames'=8,'chan'=4] {'chan'}, dimensions={1}, use_global_device_ids=true | all-gather | bytes 327680 | tf_op jit(solution)/shard_map/all_gather | solution.py:36
  24.1 2.2 %reduce = bf16[512,256]{1,0:T(8,128)(2,1)S(1)} reduce(bf16[512,1,1,256]{3,2,1,0:T(2,128)(2,1)S(1)} %bitcast.212, bf16[]{:T(256)} %broadcast.35), dimensions={1,2}, to_apply=%bitcast.179.reduce_sub_computation | reduce | bytes 524290
  27.1 3.7 %all-to-all-start = ((bf16[8,2,8192]{2,1,0:T(2,128)(2,1)}), bf16[8,2,8192]{2,1,0:T(2,128)(2,1)S(1)}, u32[]{:S(2)}, u32[]{:S(2)}) async-start(bf16[8,2,8192]{2,1,0:T(2,128)(2,1)} %reshape.84), calls=%async_computation | async-start | bytes 524288 | tf_op jit(solution)/shard_map/all_to_all | solution.py:46
  32.1 1.5 reshape.86
  33.6 4.1 %all-to-all-done = bf16[8,2,8192]{2,1,0:T(2,128)(2,1)S(1)} async-done(((bf16[8,2,8192]{2,1,0:T(2,128)(2,1)}), bf16[8,2,8192]{2,1,0:T(2,128)(2,1)S(1)}, u32[]{:S(2)}, u32[]{:S(2)}) %all-to-all-start) | async-done | bytes 262176 | tf_op jit(solution)/shard_map/all_to_all | solution.py:46
  37.7 3.5 %all-to-all-start.2 = ((bf16[8,2,16384]{2,1,0:T(2,128)(2,1)}), bf16[8,2,16384]{2,1,0:T(2,128)(2,1)S(1)}, u32[]{:S(2)}, u32[]{:S(2)}) async-start(bf16[8,2,16384]{2,1,0:T(2,128)(2,1)} %reshape.86), calls=%async_computation.2 | async-start | bytes 1048576 | tf_op jit(solution)/shard_map/all_to_all | solution.py:45
  44.0 2.1 %add_convert_fusion = bf16[16,256,256]{2,1,0:T(8,128)(2,1)} fusion(f32[16,256,256]{2,1,0:T(8,128)S(1)} %fusion.22, f32[16,256,256]{2,1,0:T(8,128)S(1)} %fusion.20, bf16[16,256,256]{1,2,0:T(8,128)(2,1)S(1)} %bitcast.202, bf16[3,256,256]{2,1,0:T(8,128)(2,1)S(1)} %copy-done.2), kind=kOutput, calls=%fused_computation.8 | convolution fusion | flops 506462208 | bytes 12713984 | tf_op jit(solution)/shard_map/fol,io->fil/dot_general | solution.py:11
  46.1 4.8 %all-to-all-done.2 = bf16[8,2,16384]{2,1,0:T(2,128)(2,1)S(1)} async-done(((bf16[8,2,16384]{2,1,0:T(2,128)(2,1)}), bf16[8,2,16384]{2,1,0:T(2,128)(2,1)S(1)}, u32[]{:S(2)}, u32[]{:S(2)}) %all-to-all-start.2) | async-done | bytes 524320 | tf_op jit(solution)/shard_map/all_to_all | solution.py:45
  50.9 4.4 %all-to-all-start.1 = ((bf16[16,256,4,64]{1,3,2,0:T(8,128)(2,1)}), bf16[16,256,4,64]{1,3,2,0:T(8,128)(2,1)}, u32[]{:S(2)}, u32[]{:S(2)}) async-start(bf16[16,256,4,64]{1,3,2,0:T(8,128)(2,1)} %bitcast.205), calls=%async_computation.1 | async-start | bytes 4194304 | tf_op jit(solution)/shard_map/all_to_all | solution.py:59
  55.5 1.2 copy.66
  56.7 1.7 reshape.87
  58.3 2.4 %copy.81 = bf16[2,64,4,8,64]{4,1,2,0,3:T(8,128)(2,1)} copy(bf16[2,64,4,8,64]{1,2,0,4,3:T(4,128)(2,1)} %bitcast.209) | data formatting | bytes 1048576 | tf_op jit(solution)/shard_map/all_to_all | solution.py:45
  60.7 3.1 %copy.82 = bf16[8,2,64,4,64]{4,3,2,1,0:T(4,128)(2,1)} copy(bf16[8,2,64,4,64]{4,2,3,1,0:T(8,128)(2,1)} %bitcast.207) | data formatting | bytes 1048576 | tf_op jit(solution)/shard_map/all_to_all | solution.py:45
  63.9 2.1 %reshape.55 = bf16[16,64,256]{2,1,0:T(8,128)(2,1)S(1)} reshape(bf16[8,2,64,4,64]{4,3,2,1,0:T(4,128)(2,1)} %copy.82) | data formatting | bytes 1048576 | tf_op jit(solution)/shard_map/reshape | solution.py:54
  65.9 1.7 %convolution_bitcast_fusion = f32[1,64,256]{2,1,0:T(8,128)S(1)} fusion(bf16[8,256,64]{1,2,0:T(8,128)(2,1)S(1)} %bitcast.214, bf16[2,64,4,8,64]{4,1,2,0,3:T(8,128)(2,1)} %copy.81), kind=kOutput, calls=%fused_computation.35 | convolution fusion | flops 134217728 | bytes 851968 | tf_op jit(solution)/shard_map/fil,fol->io/dot_general | solution.py:19
  69.4 12.5 %all-to-all-done.1 = bf16[16,256,4,64]{1,3,2,0:T(8,128)(2,1)} async-done(((bf16[16,256,4,64]{1,3,2,0:T(8,128)(2,1)}), bf16[16,256,4,64]{1,3,2,0:T(8,128)(2,1)}, u32[]{:S(2)}, u32[]{:S(2)}) %all-to-all-start.1) | async-done | bytes 2097184 | tf_op jit(solution)/shard_map/all_to_all | solution.py:59
  81.9 5.1 %copy.63 = bf16[2,256,8,2,64,2]{1,0,5,4,3,2:T(2,128)(2,1)} copy(bf16[2,256,8,2,64,2]{1,4,5,3,0,2:T(8,128)(2,1)} %bitcast.17) | data formatting | bytes 4194304 | tf_op jit(solution)/shard_map/transpose | solution.py:60
  87.0 5.1 %copy.64 = bf16[2,256,16,128]{3,1,2,0:T(8,128)(2,1)S(1)} copy(bf16[2,256,16,128]{1,0,3,2:T(2,128)(2,1)} %bitcast.206) | data formatting | bytes 4194304 | tf_op jit(solution)/shard_map/reshape | solution.py:63
  101.4 0.9 fusion.13
  103.9 0.9 pad_maximum_fusion
  106.1 1.1 copy.85
  107.2 53.1 %all-reduce.7.cloned.1.call-done = (f32[3,3,64,256]{3,2,1,0:T(8,128)}, f32[3,64,256]{2,1,0:T(8,128)}) async-done(((f32[3,3,64,256]{3,2,1,0:T(8,128)}, f32[3,64,256]{2,1,0:T(8,128)}), (f32[3,3,64,256]{3,2,1,0:T(8,128)}, f32[3,64,256]{2,1,0:T(8,128)})) %all-reduce.7.cloned.1.call-update) | async-done | bytes 786448 | tf_op jit(solution)/shard_map/psum | solution.py:88
  160.3 1.9 %broadcast_multiply_fusion = f32[3,3,64,256]{3,2,1,0:T(8,128)} fusion(f32[3,3,64,256]{3,2,1,0:T(8,128)} %get-tuple-element.15), kind=kLoop, calls=%fused_computation.50 | loop fusion | flops 147456 | bytes 1179648 | tf_op jit(solution)/shard_map/mul | solution.py:89
  162.3 1.6 broadcast_multiply_fusion.1
  (42 shorter events, 19.8 us)
Async XLA Ops:
  7.2 23.7 %copy-start.1 = (bf16[2,64,16,128]{3,2,1,0:T(8,128)(2,1)S(1)}, bf16[2,64,16,128]{3,2,1,0:T(8,128)(2,1)}, u32[]{:S(2)}) copy-start(bf16[2,64,16,128]{3,2,1,0:T(8,128)(2,1)} %param.6) | copy-start | bytes 1572868
  27.1 10.6 %all-to-all-start = ((bf16[8,2,8192]{2,1,0:T(2,128)(2,1)}), bf16[8,2,8192]{2,1,0:T(2,128)(2,1)S(1)}, u32[]{:S(2)}, u32[]{:S(2)}) async-start(bf16[8,2,8192]{2,1,0:T(2,128)(2,1)} %reshape.84), calls=%async_computation | async-start | bytes 524288 | tf_op jit(solution)/shard_map/all_to_all | solution.py:46
  37.7 13.2 %all-to-all-start.2 = ((bf16[8,2,16384]{2,1,0:T(2,128)(2,1)}), bf16[8,2,16384]{2,1,0:T(2,128)(2,1)S(1)}, u32[]{:S(2)}, u32[]{:S(2)}) async-start(bf16[8,2,16384]{2,1,0:T(2,128)(2,1)} %reshape.86), calls=%async_computation.2 | async-start | bytes 1048576 | tf_op jit(solution)/shard_map/all_to_all | solution.py:45
  41.5 1.0 copy-start.2
  50.9 31.0 %all-to-all-start.1 = ((bf16[16,256,4,64]{1,3,2,0:T(8,128)(2,1)}), bf16[16,256,4,64]{1,3,2,0:T(8,128)(2,1)}, u32[]{:S(2)}, u32[]{:S(2)}) async-start(bf16[16,256,4,64]{1,3,2,0:T(8,128)(2,1)} %bitcast.205), calls=%async_computation.1 | async-start | bytes 4194304 | tf_op jit(solution)/shard_map/all_to_all | solution.py:59
  55.2 105.1 %all-reduce.7.cloned.1.call-start = ((), (), s32[]{:S(2)}) async-start(), calls=%async_computation.3 | async-start | bytes 1572864 | tf_op jit(solution)/shard_map/psum | solution.py:88
  94.3 1.5 copy-start
  97.4 1.5 copy-start.3
Sparse Core Ops, SparseCore 0:
  104.9 55.3 all-reduce.6
where the time goes:
time: 172 us; the launch traced here: 171 us
  waiting for transfers between devices  74.6 us (43%)
  local copies, waits for them, and re-layouts  27.5 us (16%)
  matrix products  19.2 us (11%)
  blocking collectives  16 us (9%)
  between operations  14.3 us (8%)
  starting transfers between devices  11.8 us (7%)
  other arithmetic  7.4 us (4%)
    psum x1, waiting for transfers between devices, shards(): spatial_total = lax.psum(spatial_part, 'frames')  53.1 us
    all_gather x1, blocking collectives, shards(): full_cot = lax.all_gather(cotangent, 'chan', axis=1, tiled=True)  16 us
    all_to_all x1, waiting for transfers between devices, shards(): lax.all_to_all(cell_grad, 'frames', split_axis=0, concat_axis=3, tiled=True)  12.5 us
    unnamed x16, local copies, waits for them, and re-layouts  8.32 us
    dot_general x9, matrix products, shards(): jnp.einsum('fihw,fohw->io', shifted, saved_grad, preferred_element_type=j...  6.84 us
    dot_general x9, matrix products, shards(): jnp.einsum('fohw,io->fihw', window, spatial_w[tap_row, tap_col], preferre...  6.16 us
    all_to_all x2, local copies, waits for them, and re-layouts, shards(): lax.all_to_all(pooled_saved, 'frames', split_axis=3, concat_axis=0, tiled...  5.53 us
    transpose x1, local copies, waits for them, and re-layouts, shards(): back_grad.reshape(frame_count, row_total, 2, 2, row_half, col_half)  5.08 us
  transfers between devices with their start and end apart: 4, of which 4 were waited for; matrix products, arithmetic and copies ran while one was open for 14% of the time, Pallas kernels for 0%

commit v1 on v0

--- a/solution.py
+++ b/solution.py
@@ -85,7 +85,11 @@
             )
         kernel_rows.append(jnp.stack(kernel_cols))
     spatial_part = jnp.stack(kernel_rows)
-    spatial_total = lax.psum(spatial_part, "frames")
+    spatial_total = spatial_part
+    for hop in (1, 2, 4):
+        spatial_total = spatial_total + lax.ppermute(
+            spatial_total, "frames", [(dev, dev ^ hop) for dev in range(8)]
+        )
     return (input_sum.astype(jnp.bfloat16), spatial_total * scale, temporal_total * scale)
 
 

time: 172 us -> 183 us (1.064)
  waiting for transfers between devices: 74.6 us -> 88.3 us
  local copies, waits for them, and re-layouts: 27.5 us -> 25.4 us
  starting transfers between devices: 11.8 us -> 13.7 us
    ppermute x0 -> x3, waiting for transfers between devices: none -> 22.9 us  [shards(): lax.ppermute(spatial_total, 'frames', [(dev, dev ^ hop) for dev in range(...]
    all_to_all x1, waiting for transfers between devices: 12.5 us -> 0.01 us  [shards(): lax.all_to_all(cell_grad, 'frames', split_axis=0, concat_axis=3, tiled=True)]
    psum x1, waiting for transfers between devices: 53.1 us -> 56.4 us  [shards(): temporal_total = lax.psum(temporal_part, 'frames')]
    all_to_all x2, local copies, waits for them, and re-layouts: 5.53 us -> 3.59 us  [shards(): lax.all_to_all(pooled_saved, 'frames', split_axis=3, concat_axis=0, tiled...]
    ppermute x0 -> x3, starting transfers between devices: none -> 1.9 us  [shards(): lax.ppermute(spatial_total, 'frames', [(dev, dev ^ hop) for dev in range(...]
    unnamed x16 -> x18, local copies, waits for them, and re-layouts: 8.32 us -> 8.2 us
  transfers between devices with their start and end apart: 4 -> 7, of which waited for: 4 -> 6; matrix products, arithmetic and copies ran while one was open for 14% -> 15% of each run, Pallas kernels for 0% -> 0%
where the time goes in v1:
time: 183 us
  waiting for transfers between devices  88.3 us (48%)
  local copies, waits for them, and re-layouts  25.4 us (14%)
  matrix products  19.2 us (10%)
  blocking collectives  16 us (9%)
  between operations  14.3 us (8%)
  starting transfers between devices  13.7 us (7%)
  other arithmetic  5.75 us (3%)
    psum x1, waiting for transfers between devices, shards(): temporal_total = lax.psum(temporal_part, 'frames')  56.4 us
    ppermute x3, waiting for transfers between devices, shards(): lax.ppermute(spatial_total, 'frames', [(dev, dev ^ hop) for dev in range(...  22.9 us
    all_gather x1, blocking collectives, shards(): full_cot = lax.all_gather(cotangent, 'chan', axis=1, tiled=True)  16 us
    unnamed x18, local copies, waits for them, and re-layouts  8.2 us
    dot_general x9, matrix products, shards(): jnp.einsum('fihw,fohw->io', shifted, saved_grad, preferred_element_type=j...  6.84 us
    dot_general x9, matrix products, shards(): jnp.einsum('fohw,io->fihw', window, spatial_w[tap_row, tap_col], preferre...  6.17 us
    reshape x1, local copies, waits for them, and re-layouts, shards(): saved_grad = back_grad.reshape(frame_count, row_total, row_count, col_count)  5.07 us
    transpose x1, local copies, waits for them, and re-layouts, shards(): back_grad.reshape(frame_count, row_total, 2, 2, row_half, col_half)  5.07 us
  transfers between devices with their start and end apart: 7, of which 6 were waited for; matrix products, arithmetic and copies ran while one was open for 15% of the time, Pallas kernels for 0%

profile of v1, /device:TPU:0, one launch (start us, length us, event | category | flops | bytes accessed | tf_op | source)
XLA Modules:
  0.0 182.7 jit_solution(14169580845108747358)
XLA Ops:
  7.2 16.0 %all_gather.3 = bf16[1,256,512]{2,1,0:T(8,128)(2,1)S(1)} all-gather(bf16[1,64,512]{2,1,0:T(8,128)(2,1)} %param.7), channel_id=1, replica_groups=mesh['frames'=8,'chan'=4] {'chan'}, dimensions={1}, use_global_device_ids=true | all-gather | bytes 327680 | tf_op jit(solution)/shard_map/all_gather | solution.py:36
  24.1 2.2 %reduce = bf16[512,256]{1,0:T(8,128)(2,1)S(1)} reduce(bf16[512,1,1,256]{3,2,1,0:T(2,128)(2,1)S(1)} %bitcast.212, bf16[]{:T(256)} %broadcast.35), dimensions={1,2}, to_apply=%bitcast.179.reduce_sub_computation | reduce | bytes 524290
  27.1 3.7 %all-to-all-start = ((bf16[8,2,8192]{2,1,0:T(2,128)(2,1)}), bf16[8,2,8192]{2,1,0:T(2,128)(2,1)S(1)}, u32[]{:S(2)}, u32[]{:S(2)}) async-start(bf16[8,2,8192]{2,1,0:T(2,128)(2,1)} %reshape.84), calls=%async_computation | async-start | bytes 524288 | tf_op jit(solution)/shard_map/all_to_all | solution.py:46
  32.1 1.5 reshape.86
  33.6 4.1 %all-to-all-done = bf16[8,2,8192]{2,1,0:T(2,128)(2,1)S(1)} async-done(((bf16[8,2,8192]{2,1,0:T(2,128)(2,1)}), bf16[8,2,8192]{2,1,0:T(2,128)(2,1)S(1)}, u32[]{:S(2)}, u32[]{:S(2)}) %all-to-all-start) | async-done | bytes 262176 | tf_op jit(solution)/shard_map/all_to_all | solution.py:46
  37.7 3.5 %all-to-all-start.2 = ((bf16[8,2,16384]{2,1,0:T(2,128)(2,1)}), bf16[8,2,16384]{2,1,0:T(2,128)(2,1)S(1)}, u32[]{:S(2)}, u32[]{:S(2)}) async-start(bf16[8,2,16384]{2,1,0:T(2,128)(2,1)} %reshape.86), calls=%async_computation.2 | async-start | bytes 1048576 | tf_op jit(solution)/shard_map/all_to_all | solution.py:45
  44.0 2.1 %add_convert_fusion = bf16[16,256,256]{2,1,0:T(8,128)(2,1)} fusion(f32[16,256,256]{2,1,0:T(8,128)S(1)} %fusion.22, f32[16,256,256]{2,1,0:T(8,128)S(1)} %fusion.20, bf16[16,256,256]{1,2,0:T(8,128)(2,1)S(1)} %bitcast.202, bf16[3,256,256]{2,1,0:T(8,128)(2,1)S(1)} %copy-done.3), kind=kOutput, calls=%fused_computation.8 | convolution fusion | flops 506462208 | bytes 12713984 | tf_op jit(solution)/shard_map/fol,io->fil/dot_general | solution.py:11
  46.1 4.8 %all-to-all-done.2 = bf16[8,2,16384]{2,1,0:T(2,128)(2,1)S(1)} async-done(((bf16[8,2,16384]{2,1,0:T(2,128)(2,1)}), bf16[8,2,16384]{2,1,0:T(2,128)(2,1)S(1)}, u32[]{:S(2)}, u32[]{:S(2)}) %all-to-all-start.2) | async-done | bytes 524320 | tf_op jit(solution)/shard_map/all_to_all | solution.py:45
  50.9 4.4 %all-to-all-start.1 = ((bf16[16,256,4,64]{1,3,2,0:T(8,128)(2,1)}), bf16[16,256,4,64]{1,3,2,0:T(8,128)(2,1)}, u32[]{:S(2)}, u32[]{:S(2)}) async-start(bf16[16,256,4,64]{1,3,2,0:T(8,128)(2,1)} %bitcast.205), calls=%async_computation.1 | async-start | bytes 4194304 | tf_op jit(solution)/shard_map/all_to_all | solution.py:59
  55.5 1.6 reshape.87
  57.1 1.7 copy.81
  58.9 1.0 copy-done
  59.8 1.9 %copy.82 = bf16[8,2,64,4,64]{4,3,2,1,0:T(4,128)(2,1)} copy(bf16[8,2,64,4,64]{4,2,3,1,0:T(8,128)(2,1)S(1)} %bitcast.207) | data formatting | bytes 1048576 | tf_op jit(solution)/shard_map/all_to_all | solution.py:45
  61.7 2.1 %reshape.55 = bf16[16,64,256]{2,1,0:T(8,128)(2,1)S(1)} reshape(bf16[8,2,64,4,64]{4,3,2,1,0:T(4,128)(2,1)} %copy.82) | data formatting | bytes 1048576 | tf_op jit(solution)/shard_map/reshape | solution.py:54
  63.8 1.7 convolution_bitcast_fusion
  67.4 56.4 %all-reduce.6.cloned.1.call-done = f32[3,64,256]{2,1,0:T(8,128)} async-done(((f32[3,64,256]{2,1,0:T(8,128)}), f32[3,64,256]{2,1,0:T(8,128)}) %all-reduce.6.cloned.1.call-update) | async-done | bytes 196624 | tf_op jit(solution)/shard_map/psum | solution.py:64
  123.8 1.6 broadcast_multiply_fusion
  125.4 5.1 %copy.63 = bf16[2,256,8,2,64,2]{1,0,5,4,3,2:T(2,128)(2,1)} copy(bf16[2,256,8,2,64,2]{1,4,5,3,0,2:T(8,128)(2,1)} %bitcast.17) | data formatting | bytes 4194304 | tf_op jit(solution)/shard_map/transpose | solution.py:60
  130.5 5.1 %copy.64 = bf16[2,256,16,128]{3,1,2,0:T(8,128)(2,1)S(1)} copy(bf16[2,256,16,128]{1,0,3,2:T(2,128)(2,1)} %bitcast.206) | data formatting | bytes 4194304 | tf_op jit(solution)/shard_map/reshape | solution.py:63
  144.7 0.9 collective-permute-start.1
  148.0 12.1 %collective-permute-done.1 = f32[3,3,64,256]{3,2,1,0:T(8,128)S(1)} collective-permute-done((f32[3,3,64,256]{3,2,1,0:T(8,128)S(1)}, f32[3,3,64,256]{3,2,1,0:T(8,128)S(1)}, u32[]{:S(2)}, u32[]{:S(2)}) %collective-permute-start.1) | collective-permute-done | bytes 589856 | tf_op jit(solution)/shard_map/ppermute | solution.py:90
  160.3 0.9 collective-permute-start.2
  163.3 1.1 copy.85
  164.4 10.5 %collective-permute-done.2 = f32[3,3,64,256]{3,2,1,0:T(8,128)S(1)} collective-permute-done((f32[3,3,64,256]{3,2,1,0:T(8,128)S(1)}, f32[3,3,64,256]{3,2,1,0:T(8,128)S(1)}, u32[]{:S(2)}, u32[]{:S(2)}) %collective-permute-start.2) | collective-permute-done | bytes 589856 | tf_op jit(solution)/shard_map/ppermute | solution.py:90
  (52 shorter events, 22.4 us)
Async XLA Ops:
  7.2 23.7 %copy-start.2 = (bf16[2,64,16,128]{3,2,1,0:T(8,128)(2,1)S(1)}, bf16[2,64,16,128]{3,2,1,0:T(8,128)(2,1)}, u32[]{:S(2)}) copy-start(bf16[2,64,16,128]{3,2,1,0:T(8,128)(2,1)} %param.6) | copy-start | bytes 1572868
  27.1 10.6 %all-to-all-start = ((bf16[8,2,8192]{2,1,0:T(2,128)(2,1)}), bf16[8,2,8192]{2,1,0:T(2,128)(2,1)S(1)}, u32[]{:S(2)}, u32[]{:S(2)}) async-start(bf16[8,2,8192]{2,1,0:T(2,128)(2,1)} %reshape.84), calls=%async_computation | async-start | bytes 524288 | tf_op jit(solution)/shard_map/all_to_all | solution.py:46
  37.7 13.2 %all-to-all-start.2 = ((bf16[8,2,16384]{2,1,0:T(2,128)(2,1)}), bf16[8,2,16384]{2,1,0:T(2,128)(2,1)S(1)}, u32[]{:S(2)}, u32[]{:S(2)}) async-start(bf16[8,2,16384]{2,1,0:T(2,128)(2,1)} %reshape.86), calls=%async_computation.2 | async-start | bytes 1048576 | tf_op jit(solution)/shard_map/all_to_all | solution.py:45
  41.5 1.0 copy-start.3
  50.9 74.5 %all-to-all-start.1 = ((bf16[16,256,4,64]{1,3,2,0:T(8,128)(2,1)}), bf16[16,256,4,64]{1,3,2,0:T(8,128)(2,1)}, u32[]{:S(2)}, u32[]{:S(2)}) async-start(bf16[16,256,4,64]{1,3,2,0:T(8,128)(2,1)} %bitcast.205), calls=%async_computation.1 | async-start | bytes 4194304 | tf_op jit(solution)/shard_map/all_to_all | solution.py:59
  55.2 68.5 %all-reduce.6.cloned.1.call-start = ((), (), s32[]{:S(2)}) async-start(), calls=%async_computation.3 | async-start | bytes 393216 | tf_op jit(solution)/shard_map/psum | solution.py:64
  58.8 1.0 copy-start
  66.0 1.2 copy-start.1
  141.6 1.0 copy-start.4
  142.5 2.1 %collective-permute-start = (f32[3,3,64,256]{3,2,1,0:T(8,128)S(1)}, f32[3,3,64,256]{3,2,1,0:T(8,128)S(1)}, u32[]{:S(2)}, u32[]{:S(2)}) collective-permute-start(f32[3,3,64,256]{3,2,1,0:T(8,128)S(1)} %pad_maximum_fusion), channel_id=1, source_target_pairs={{0,4},{4,0},{8,12},{12,8},{16,20},{20,16},{24,28},{28,24},{1,5},{5... | collective-permute-start | bytes 1769480 | tf_op jit(solution)/shard_map/ppermute | solution.py:90
  144.7 15.5 %collective-permute-start.1 = (f32[3,3,64,256]{3,2,1,0:T(8,128)S(1)}, f32[3,3,64,256]{3,2,1,0:T(8,128)S(1)}, u32[]{:S(2)}, u32[]{:S(2)}) collective-permute-start(f32[3,3,64,256]{3,2,1,0:T(8,128)S(1)} %fusion.64), channel_id=1, source_target_pairs={{0,8},{4,12},{8,0},{12,4},{16,24},{20,28},{24,16},{28,20},{1,9},{5... | collective-permute-start | bytes 1769480 | tf_op jit(solution)/shard_map/ppermute | solution.py:90
  160.3 14.6 %collective-permute-start.2 = (f32[3,3,64,256]{3,2,1,0:T(8,128)S(1)}, f32[3,3,64,256]{3,2,1,0:T(8,128)S(1)}, u32[]{:S(2)}, u32[]{:S(2)}) collective-permute-start(f32[3,3,64,256]{3,2,1,0:T(8,128)S(1)} %fusion.82), channel_id=1, source_target_pairs={{0,16},{4,20},{8,24},{12,28},{16,0},{20,4},{24,8},{28,12},{1,17},{... | collective-permute-start | bytes 1769480 | tf_op jit(solution)/shard_map/ppermute | solution.py:90
Sparse Core Ops, SparseCore 0:
  67.3 56.3 all-reduce.5
